TPU v7x, 512 devices: a whole 4x8x8 slice. The times are simulated.
512 devices in a mesh: section: 4 (over x), rep: 128 (over y, z, core).
Axes of the slice: x: 4, y: 8, z: 8, core: 2. Of those that a mesh axis runs over, the one named last changes fastest.
Arguments:
- tile_features: bfloat16 [256, 16, 16, 512], P('rep'), may hold values from -6 to 6
- patches: bfloat16 [256, 16, 16, 768], P('rep'), may hold values from -6 to 6
- det_kernel: float32 [4, 7, 7, 512], P('section'), may hold values from -0.875 to 0.875
- det_gain: float32 [4, 512], P('section'), may hold values from 0.1 to 1.9
- det_in: bfloat16 [4, 512, 2048], P('section', None, 'rep'), may hold values from -0.25 to 0.25
- det_out: bfloat16 [4, 2048, 512], P('section', 'rep'), may hold values from -0.125 to 0.125
- det_scale: float32 [4, 512], P('section'), may hold values from 0.3 to 1.5
- cls_embed: bfloat16 [768, 1024], P(None, 'section'), may hold values from -0.21875 to 0.21875
- cls_merge: bfloat16 [512, 1024], P(None, 'section'), may hold values from -0.25 to 0.25
- cls_pos: bfloat16 [196, 1024], P(None, 'section'), may hold values from -3 to 3
- cls_qkv: bfloat16 [1024, 3, 512], P(None, None, 'section'), may hold values from -1.5 to 1.5
- cls_out: bfloat16 [512, 1024], P('section'), may hold values from -0.25 to 0.25
- cls_gain: float32 [2, 1024], replicated, may hold values from 0.1 to 1.9
- crop_plan: int32 [128, 4, 3, 3], P('rep'), may hold values from 0 to 2, as said below
- slot_from: int32 [128, 4], P('rep'), may hold values from 0 to 3, as said below
Outputs:
- crop_class: float32 [128, 4, 1024], P('rep', 'section')
Inputs may be any that keep to these rules, and one draw needn't show every extreme that they name: `crop_plan`: each entry is a micro-batch below 2 followed by a top and a left patch offset of 0 to 2; records that no slot names are arbitrary. `slot_from`: 0 marks an empty slot, 1 a crop from the replica one index lower, 2 the replica's own, 3 one from the replica one index higher; the first replica never has 1 and the last never has 3.
All inputs are finite; a program needn't handle non-finite values.
Results may differ from a plain program's by a relative error of at most 0.004.
Values may be sent and summed in bfloat16 or wider, within the bound.
No kernel may reach another device: no remote copies, remote signals or barrier semaphores. Data moves between devices by JAX's collectives and lax.ppermute only.
A program may use at most 64 MiB of HBM per device.

v0:
```python
import math
import jax
import jax.numpy as jnp
from jax import lax
from jax.sharding import PartitionSpec as P

HEAD_DIM = 64
TILE = 16
CROP = 14
epsilon = 1e-06


def passed_along(block, axis, distance):
    devices = range(lax.axis_size(axis))
    route = [(i - distance, i) for i in devices if i - distance in devices]
    return lax.ppermute(block, axis, route)


def spread(value, axis, source):
    kept = jnp.where(lax.axis_index(axis) == source, value, 0).astype(value.dtype)
    return lax.psum(kept, axis)


def padded_2(block, sides, width):
    for axis, dim in sides:
        count = lax.axis_size(axis)
        forward = [(i, i + 1) for i in range(count - 1)]
        backward = [(target, source) for source, target in forward]
        low = lax.ppermute(
            lax.slice_in_dim(block, block.shape[dim] - width, None, axis=dim), axis, forward
        )
        high = lax.ppermute(lax.slice_in_dim(block, 0, width, axis=dim), axis, backward)
        block = jnp.concatenate([low, block, high], axis=dim)
    return block


def layer_norm(values, gain_row):
    row_mean = jnp.mean(values, axis=-1, keepdims=True)
    centred = values - row_mean
    row_var = jnp.mean(centred * centred, axis=-1, keepdims=True)
    return centred * lax.rsqrt(row_var + epsilon) * gain_row


def detector_block(tile_rows, kernel, gain_row, in_weight, out_weight, scale_row):
    widened = tile_rows.astype(jnp.float32)
    padded = jnp.pad(widened, ((3, 3), (3, 3), (0, 0)))
    conv = jnp.zeros_like(widened)
    for row_shift in range(7):
        for col_shift in range(7):
            conv = (
                conv
                + padded[row_shift : row_shift + TILE, col_shift : col_shift + TILE]
                * kernel[row_shift, col_shift]
            )
    normed = layer_norm(conv, gain_row).astype(jnp.bfloat16).reshape(TILE * TILE, -1)
    hidden = jax.nn.gelu(jnp.dot(normed, in_weight, preferred_element_type=jnp.float32)).astype(
        jnp.bfloat16
    )
    update = jnp.dot(hidden, out_weight, preferred_element_type=jnp.float32).reshape(widened.shape)
    return (widened + scale_row * update).astype(jnp.bfloat16)


def per_device(
    tile_features,
    patches,
    det_kernel,
    det_gain,
    det_in,
    det_out,
    det_scale,
    cls_embed,
    cls_merge,
    cls_pos,
    cls_qkv,
    cls_out,
    cls_gain,
    crop_plan,
    slot_from,
):
    sections = lax.axis_size("section")
    section_num = lax.axis_index("section")
    micro_count = tile_features.shape[0]
    in_whole, out_whole = (
        lax.all_gather(det_in, "rep", axis=2, tiled=True),
        lax.all_gather(det_out, "rep", axis=1, tiled=True),
    )
    kernel = det_kernel[0]
    gain_row = det_gain[0]
    scale_row = det_scale[0]
    in_weight = in_whole[0]
    out_weight = out_whole[0]

    def run_block(operand_tile):
        return detector_block(operand_tile, kernel, gain_row, in_weight, out_weight, scale_row)

    def skip_block(operand_tile):
        return jnp.zeros_like(operand_tile)

    def tick(tick_index, loop_state):
        incoming, finals = loop_state
        micro_num = tick_index - section_num
        is_valid = (micro_num >= 0) & (micro_num < micro_count)
        clipped = jnp.clip(micro_num, 0, micro_count - 1)
        fresh_tile = lax.dynamic_index_in_dim(tile_features, clipped, 0, keepdims=False)
        operand = jnp.where(section_num == 0, fresh_tile, incoming)
        result = lax.cond(is_valid, run_block, skip_block, operand)
        stored = lax.dynamic_update_index_in_dim(finals, result, clipped, 0)
        finals = jnp.where(is_valid & (section_num == sections - 1), stored, finals)
        incoming = passed_along(result, "section", 1)
        return (incoming, finals)

    start_state = (
        jnp.zeros(tile_features.shape[1:], jnp.bfloat16),
        jnp.zeros(tile_features.shape, jnp.bfloat16),
    )
    unused_tile, finals = lax.fori_loop(0, micro_count + sections - 1, tick, start_state)
    finals = spread(finals, "section", sections - 1)
    pixel_width = patches.shape[3]
    feat_width = finals.shape[3]
    full_width = cls_gain.shape[1]
    local_width = cls_embed.shape[1]
    local_heads = cls_qkv.shape[2] // HEAD_DIM
    qkv_flat = cls_qkv.reshape(cls_qkv.shape[0], -1)
    gain_first = lax.dynamic_slice_in_dim(cls_gain[0], section_num * local_width, local_width)
    slot_plan = crop_plan[0]
    source = lax.dynamic_index_in_dim(slot_from[0], section_num, 0, keepdims=False)
    zero_index = jnp.int32(0)

    def cut_crop(record):
        pixel_rows = lax.dynamic_slice(
            patches, (record[0], record[1], record[2], zero_index), (1, CROP, CROP, pixel_width)
        ).reshape(CROP * CROP, pixel_width)
        feat_rows = lax.dynamic_slice(
            finals, (record[0], record[1], record[2], zero_index), (1, CROP, CROP, feat_width)
        ).reshape(CROP * CROP, feat_width)
        return (pixel_rows, feat_rows)

    pixel_rows, feat_rows = jax.vmap(cut_crop)(slot_plan.reshape(-1, 3))
    count = pixel_rows.shape[0]
    widened = (
        jnp.einsum("crp,pd->crd", pixel_rows, cls_embed, preferred_element_type=jnp.float32)
        + jnp.einsum("crp,pd->crd", feat_rows, cls_merge, preferred_element_type=jnp.float32)
        + cls_pos.astype(jnp.float32)[None]
    )
    row_sum, row_square = lax.psum(
        (jnp.sum(widened, axis=-1), jnp.sum(widened * widened, axis=-1)), "section"
    )
    row_mean = row_sum / full_width
    row_var = row_square / full_width - row_mean * row_mean
    attn_part = (
        (widened - row_mean[..., None]) * lax.rsqrt(row_var[..., None] + epsilon) * gain_first
    ).astype(jnp.bfloat16)
    attn_in = lax.all_gather(attn_part, "section", axis=2, tiled=True)
    qkv = jnp.einsum("crd,de->cre", attn_in, qkv_flat, preferred_element_type=jnp.float32).astype(
        jnp.bfloat16
    )
    qkv = qkv.reshape(count, CROP * CROP, 3, local_heads, HEAD_DIM)
    query_rows = qkv[:, :, 0]
    key_rows = qkv[:, :, 1]
    value_rows = qkv[:, :, 2]
    scores = jnp.einsum(
        "cqhd,ckhd->chqk", query_rows, key_rows, preferred_element_type=jnp.float32
    ) * (1.0 / math.sqrt(HEAD_DIM))
    top_score = jnp.max(scores, axis=-1, keepdims=True)
    weights = jnp.exp(scores - top_score)
    probs = (weights / jnp.sum(weights, axis=-1, keepdims=True)).astype(jnp.bfloat16)
    context = jnp.einsum(
        "chqk,ckhd->cqhd", probs, value_rows, preferred_element_type=jnp.float32
    ).astype(jnp.bfloat16)
    context_mean = jnp.mean(context.reshape(count, CROP * CROP, -1).astype(jnp.float32), axis=1)
    context_term = jnp.dot(
        context_mean, cls_out.astype(jnp.float32), precision=lax.Precision.HIGHEST
    )
    token_mean = jnp.mean(widened, axis=1)
    placed = lax.dynamic_update_slice_in_dim(
        jnp.zeros((count, full_width), jnp.float32), token_mean, section_num * local_width, 1
    )
    terms = (placed + context_term).reshape(sections, -1)
    pooled = lax.psum_scatter(terms, "section", scatter_dimension=0, tiled=True).reshape(
        -1, full_width
    )
    results = layer_norm(pooled, cls_gain[1])
    outgoing_results = jnp.stack([results[0], results[2]], axis=0)
    extended_results = padded_2(outgoing_results, (("rep", 0),), 1)
    result = jnp.where(
        source == 1, extended_results[0], jnp.where(source == 3, extended_results[3], results[1])
    )
    result = jnp.where(source == 0, jnp.zeros_like(result), result)
    return result[None, None, :]


def solution(mesh):
    return jax.shard_map(
        per_device,
        mesh=mesh,
        in_specs=(
            P("rep", None, None, None),
            P("rep", None, None, None),
            P("section", None, None, None),
            P("section", None),
            P("section", None, "rep"),
            P("section", "rep", None),
            P("section", None),
            P(None, "section"),
            P(None, "section"),
            P(None, "section"),
            P(None, None, "section"),
            P("section", None),
            P(),
            P("rep", None, None, None),
            P("rep", None),
        ),
        out_specs=P("rep", "section", None),
        check_vma=False,
    )
```

profile of v0, /device:TPU:32, one launch (start us, length us, event | category | flops | bytes accessed | tf_op | source)
XLA Modules:
  0.0 480.8 jit_solution(15910834706224890067)
XLA Ops:
  9.9 52.1 %while.18 = (s32[]{:T(128)}, bf16[2,16,16,768]{3,2,1,0:T(8,128)(2,1)}, s32[12,4]{0,1:T(4,128)S(1)}, bf16[12,1,14,14,768]{4,3,2,1,0:T(8,128)(2,1)}, s32[]{:T(128)}) while((s32[]{:T(128)}, bf16[2,16,16,768]{3,2,1,0:T(8,128)(2,1)}, s32[12,4]{0,1:T(4,128)S(1)}, bf16[12,1,14,14,768]{4,3,2,1,0:T(8,128)(2,1)}, s32[]{:T(128)}) %tuple.126), condition=%wide.while_cond, body=%wide.while_body.sunk | while | flops 2 | bytes 690297 | solution.py:130
  62.0 34.7 %all-gather.4.cloned.1.call-done = bf16[1,512,2048]{1,2,0:T(8,128)(2,1)} async-done(((bf16[1,512,16]{1,2,0:T(8,128)(2,1)}), bf16[1,512,2048]{1,2,0:T(8,128)(2,1)}) %all-gather.4.cloned.1.call-update) | async-done | bytes 2097168 | tf_op jit(solution)/shard_map/all_gather | solution.py:84
  100.7 79.0 %all-gather.6.cloned.1.call-done = bf16[1,2048,512]{2,1,0:T(8,128)(2,1)} async-done(((bf16[1,16,512]{2,1,0:T(8,128)(2,1)}), bf16[1,2048,512]{2,1,0:T(8,128)(2,1)}) %all-gather.6.cloned.1.call-update) | async-done | bytes 2097168 | tf_op jit(solution)/shard_map/all_gather | solution.py:85
  179.7 84.6 %while.17 = (s32[]{:T(128)}, bf16[16,16,512]{2,1,0:T(8,128)(2,1)S(1)}, bf16[2,16,16,512]{3,2,1,0:T(8,128)(2,1)S(1)}, s32[]{:T(128)}, pred[]{:T(512)}, /*index=5*...) while((s32[]{:T(128)}, ...), condition=%wide.region_5.6_spmd, body=%wide.region_0.5_spmd.sunk | while | flops 1093009664 | bytes 12373336 | solution.py:116
  179.8 10.3 %conditional.2 = (bf16[16,16,512]{2,1,0:T(8,128)(2,1)}, bf16[1,16,16,512]{3,2,1,0:T(8,128)(2,1)S(1)}) conditional(s32[]{:T(128)} %convert_element_type.74, () %tuple.120, (pred[]{:T(512)}, bf16[2,16,16,512]{3,2,1,0:T(8,128)(2,1)S(1)}, s32[]{:T(128)}, bf16[16,16,512]{2,1,0:T(8,128)(2,1)S(1)}, f32[1,512]{1,0:T(1,128)S(1)}, ...), branch_computations={%region_1.1_spmd, %region_2.4_spmd} | conditional | flops 1092878592 | bytes 10538005 | solution.py:106
  180.0 4.2 fusion.129
  191.5 6.5 %collective-permute-done = bf16[16,16,512]{2,1,0:T(8,128)(2,1)S(1)} collective-permute-done((bf16[16,16,512]{2,1,0:T(8,128)(2,1)}, bf16[16,16,512]{2,1,0:T(8,128)(2,1)S(1)}, u32[]{:S(2)}, u32[]{:S(2)}) %collective-permute-start) | collective-permute-done | bytes 262176 | tf_op jit(solution)/shard_map/while/body/eval_jaxpr/ppermute | solution.py:16
  198.0 10.3 %conditional.2 = (bf16[16,16,512]{2,1,0:T(8,128)(2,1)}, bf16[1,16,16,512]{3,2,1,0:T(8,128)(2,1)S(1)}) conditional(s32[]{:T(128)} %convert_element_type.74, () %tuple.120, (pred[]{:T(512)}, bf16[2,16,16,512]{3,2,1,0:T(8,128)(2,1)S(1)}, s32[]{:T(128)}, bf16[16,16,512]{2,1,0:T(8,128)(2,1)S(1)}, f32[1,512]{1,0:T(1,128)S(1)}, ...), branch_computations={%region_1.1_spmd, %region_2.4_spmd} | conditional | flops 1092878592 | bytes 10538005 | solution.py:106
  198.1 4.2 fusion.129
  208.3 4.3 collective-permute-start
  212.7 5.7 %collective-permute-done = bf16[16,16,512]{2,1,0:T(8,128)(2,1)S(1)} collective-permute-done((bf16[16,16,512]{2,1,0:T(8,128)(2,1)}, bf16[16,16,512]{2,1,0:T(8,128)(2,1)S(1)}, u32[]{:S(2)}, u32[]{:S(2)}) %collective-permute-start) | collective-permute-done | bytes 262176 | tf_op jit(solution)/shard_map/while/body/eval_jaxpr/ppermute | solution.py:16
  219.2 13.9 %collective-permute-start = (bf16[16,16,512]{2,1,0:T(8,128)(2,1)}, bf16[16,16,512]{2,1,0:T(8,128)(2,1)S(1)}, u32[]{:S(2)}, u32[]{:S(2)}) collective-permute-start(bf16[16,16,512]{2,1,0:T(8,128)(2,1)} %get-tuple-element.531), channel_id=1, source_target_pairs={{0,128},{128,256},{256,384},{1,129},{129,257},{257,385},{2,130},{1... | collective-permute-start | bytes 786440 | tf_op jit(solution)/shard_map/while/body/eval_jaxpr/ppermute | solution.py:16
  233.1 4.8 %collective-permute-done = bf16[16,16,512]{2,1,0:T(8,128)(2,1)S(1)} collective-permute-done((bf16[16,16,512]{2,1,0:T(8,128)(2,1)}, bf16[16,16,512]{2,1,0:T(8,128)(2,1)S(1)}, u32[]{:S(2)}, u32[]{:S(2)}) %collective-permute-start) | collective-permute-done | bytes 262176 | tf_op jit(solution)/shard_map/while/body/eval_jaxpr/ppermute | solution.py:16
  238.7 4.3 collective-permute-start
  247.9 12.2 %collective-permute-start = (bf16[16,16,512]{2,1,0:T(8,128)(2,1)}, bf16[16,16,512]{2,1,0:T(8,128)(2,1)S(1)}, u32[]{:S(2)}, u32[]{:S(2)}) collective-permute-start(bf16[16,16,512]{2,1,0:T(8,128)(2,1)} %get-tuple-element.531), channel_id=1, source_target_pairs={{0,128},{128,256},{256,384},{1,129},{129,257},{257,385},{2,130},{1... | collective-permute-start | bytes 786440 | tf_op jit(solution)/shard_map/while/body/eval_jaxpr/ppermute | solution.py:16
  266.1 6.0 %reshape.115 = bf16[12,196,768]{2,1,0:T(8,128)(2,1)} reshape(bf16[12,1,14,14,768]{4,3,2,1,0:T(8,128)(2,1)} %get-tuple-element.289) | data formatting | bytes 7225344 | tf_op jit(solution)/shard_map/vmap()/reshape | solution.py:132
  275.3 52.9 %all-reduce.5.cloned.1.call-done = bf16[2,16,16,512]{3,0,2,1:T(2,128)(2,1)} async-done(((bf16[2,16,16,512]{3,0,2,1:T(2,128)(2,1)}), bf16[2,16,16,512]{3,0,2,1:T(2,128)(2,1)}) %all-reduce.5.cloned.1.call-update) | async-done | bytes 524304 | tf_op jit(solution)/shard_map/psum | solution.py:21
  328.2 12.1 %gather_fusion = bf16[12,14,14,512]{3,0,2,1:T(8,128)(2,1)} fusion(bf16[2,16,16,512]{3,0,2,1:T(2,128)(2,1)} %all-reduce.5.cloned.1.call-done, s32[12]{0:T(128)S(1)} %get-tuple-element.423), kind=kCustom, calls=%fused_computation | custom fusion | bytes 4817088 | tf_op jit(solution)/shard_map/vmap()/gather | solution.py:133
  340.3 6.5 %fusion.128 = (f32[12,256]{1,0:T(8,128)S(1)}, f32[12,196]{1,0:T(8,128)S(1)}, f32[12,196]{1,0:T(8,128)S(1)}, f32[12,196,256]{2,1,0:T(8,128)}) fusion(f32[196,256]{1,0:T(8,128)S(1)} %convert_element_type.50, f32[12,196,256]{2,1,0:T(8,128)S(1)} %fusion.123, bf16[512,256]{1,0:T(8,128)(2,1)S(1)} %copy-done.9, bf16[12,196,512]{2,0,1:T(8,128)(2,1)} %bitcast.131), kind=kOutput, calls=%fused_computation.214 | convolution fusion | flops 620167552 | bytes 7719296 | tf_op jit(solution)/shard_map/crp,pd->crd/dot_general | solution.py:142
  346.7 16.1 %all-reduce.2 = (f32[12,196]{1,0:T(8,128)S(1)}, f32[12,196]{1,0:T(8,128)S(1)}) all-reduce(f32[12,196]{1,0:T(8,128)S(1)} %get-tuple-element.327, f32[12,196]{1,0:T(8,128)S(1)} %get-tuple-element.328), channel_id=1, replica_groups=mesh['section'=4,'rep'=128] {'section'}, use_global_device_ids=true, to_apply=%region_10.11 | all-reduce | flops 4704 | bytes 37632 | tf_op jit(solution)/shard_map/psum | solution.py:145
  367.5 61.6 %all-gather.8.cloned.1.call-done = bf16[12,196,1024]{2,1,0:T(8,128)(2,1)} async-done(((bf16[12,196,256]{2,1,0:T(8,128)(2,1)}), bf16[12,196,1024]{2,1,0:T(8,128)(2,1)}) %all-gather.8.cloned.1.call-update) | async-done | bytes 4816912 | tf_op jit(solution)/shard_map/all_gather | solution.py:153
  429.1 6.4 %convolution_convert_fusion = bf16[12,196,384]{2,1,0:T(8,128)(2,1)} fusion(bf16[12,196,1024]{2,1,0:T(8,128)(2,1)} %all-gather.8.cloned.1.call-done, bf16[1024,384,1]{0,1,2:T(8,128)(2,1)S(1)} %bitcast.133), kind=kOutput, calls=%fused_computation.181 | convolution fusion | flops 1850591232 | bytes 7409664 | tf_op jit(solution)/shard_map/crd,de->cre/dot_general | solution.py:154
  444.5 16.7 %all-reduce.1 = f32[4,3072]{1,0:T(4,128)S(1)} all-reduce(f32[4,3072]{1,0:T(4,128)S(1)} %reshape.119), channel_id=2, replica_groups=mesh['section'=4,'rep'=128] {'section'}, use_global_device_ids=true, to_apply=%region_15.16.clone | all-reduce | flops 12288 | bytes 98304
  464.3 7.0 %collective-permute-start.2 = (f32[1,1024]{1,0:T(1,128)S(1)}, f32[1,1024]{1,0:T(1,128)S(1)}, u32[]{:S(2)}, u32[]{:S(2)}) collective-permute-start(f32[1,1024]{1,0:T(1,128)S(1)} %get-tuple-element.417), channel_id=1, source_target_pairs={{1,0},{2,1},{3,2},{4,3},{5,4},{6,5},{7,6},{8,7},{9,8},{10,9},{11,1... | collective-permute-start | bytes 12296 | tf_op jit(solution)/shard_map/ppermute | solution.py:32
  (144 shorter events, 109.2 us)
Async XLA Ops:
  6.5 265.6 %copy-start = (bf16[768,256]{1,0:T(8,128)(2,1)S(1)}, bf16[768,256]{1,0:T(8,128)(2,1)}, u32[]{:S(2)}) copy-start(bf16[768,256]{1,0:T(8,128)(2,1)} %param.26) | copy-start | bytes 1179652
  6.5 90.1 %all-gather.4.cloned.1.call-start = ((), (), s32[]{:S(2)}) async-start(), calls=%async_computation | async-start | bytes 2113536 | tf_op jit(solution)/shard_map/all_gather | solution.py:84
  7.3 172.4 %all-gather.6.cloned.1.call-start = ((), (), s32[]{:S(2)}) async-start(), calls=%async_computation.1 | async-start | bytes 2113536 | tf_op jit(solution)/shard_map/all_gather | solution.py:85
  8.0 320.2 %all-reduce.5.cloned.1.call-start = ((), (), s32[]{:S(2)}) async-start(), calls=%async_computation.2 | async-start | bytes 1048576 | tf_op jit(solution)/shard_map/psum | solution.py:21
  96.7 83.1 %copy-start.1 = (bf16[2,16,16,512]{3,2,1,0:T(8,128)(2,1)S(1)}, bf16[2,16,16,512]{3,2,1,0:T(8,128)(2,1)}, u32[]{:S(2)}) copy-start(bf16[2,16,16,512]{3,2,1,0:T(8,128)(2,1)} %param.19) | copy-start | bytes 1572868
  96.7 83.1 %copy-start.5 = (f32[1,512]{1,0:T(1,128)S(1)}, f32[1,512]{1,0:T(1,128)}, u32[]{:S(2)}) copy-start(f32[1,512]{1,0:T(1,128)} %param.25) | copy-start | bytes 6148
  96.7 83.1 %copy-start.6 = (f32[1,512]{1,0:T(1,128)S(1)}, f32[1,512]{1,0:T(1,128)}, u32[]{:S(2)}) copy-start(f32[1,512]{1,0:T(1,128)} %param.22) | copy-start | bytes 6148
  179.7 86.3 %copy-start.7 = (f32[2,1024]{1,0:T(2,128)S(1)}, f32[2,1024]{1,0:T(2,128)}, u32[]{:S(2)}) copy-start(f32[2,1024]{1,0:T(2,128)} %param.31) | copy-start | bytes 24580
  190.1 7.9 %collective-permute-start = (bf16[16,16,512]{2,1,0:T(8,128)(2,1)}, bf16[16,16,512]{2,1,0:T(8,128)(2,1)S(1)}, u32[]{:S(2)}, u32[]{:S(2)}) collective-permute-start(bf16[16,16,512]{2,1,0:T(8,128)(2,1)} %get-tuple-element.531), channel_id=1, source_target_pairs={{0,128},{128,256},{256,384},{1,129},{129,257},{257,385},{2,130},{1... | collective-permute-start | bytes 786440 | tf_op jit(solution)/shard_map/while/body/eval_jaxpr/ppermute | solution.py:16
  208.3 10.1 %collective-permute-start = (bf16[16,16,512]{2,1,0:T(8,128)(2,1)}, bf16[16,16,512]{2,1,0:T(8,128)(2,1)S(1)}, u32[]{:S(2)}, u32[]{:S(2)}) collective-permute-start(bf16[16,16,512]{2,1,0:T(8,128)(2,1)} %get-tuple-element.531), channel_id=1, source_target_pairs={{0,128},{128,256},{256,384},{1,129},{129,257},{257,385},{2,130},{1... | collective-permute-start | bytes 786440 | tf_op jit(solution)/shard_map/while/body/eval_jaxpr/ppermute | solution.py:16
  219.2 18.8 %collective-permute-start = (bf16[16,16,512]{2,1,0:T(8,128)(2,1)}, bf16[16,16,512]{2,1,0:T(8,128)(2,1)S(1)}, u32[]{:S(2)}, u32[]{:S(2)}) collective-permute-start(bf16[16,16,512]{2,1,0:T(8,128)(2,1)} %get-tuple-element.531), channel_id=1, source_target_pairs={{0,128},{128,256},{256,384},{1,129},{129,257},{257,385},{2,130},{1... | collective-permute-start | bytes 786440 | tf_op jit(solution)/shard_map/while/body/eval_jaxpr/ppermute | solution.py:16
  238.7 8.5 %collective-permute-start = (bf16[16,16,512]{2,1,0:T(8,128)(2,1)}, bf16[16,16,512]{2,1,0:T(8,128)(2,1)S(1)}, u32[]{:S(2)}, u32[]{:S(2)}) collective-permute-start(bf16[16,16,512]{2,1,0:T(8,128)(2,1)} %get-tuple-element.531), channel_id=1, source_target_pairs={{0,128},{128,256},{256,384},{1,129},{129,257},{257,385},{2,130},{1... | collective-permute-start | bytes 786440 | tf_op jit(solution)/shard_map/while/body/eval_jaxpr/ppermute | solution.py:16
  247.9 16.4 %collective-permute-start = (bf16[16,16,512]{2,1,0:T(8,128)(2,1)}, bf16[16,16,512]{2,1,0:T(8,128)(2,1)S(1)}, u32[]{:S(2)}, u32[]{:S(2)}) collective-permute-start(bf16[16,16,512]{2,1,0:T(8,128)(2,1)} %get-tuple-element.531), channel_id=1, source_target_pairs={{0,128},{128,256},{256,384},{1,129},{129,257},{257,385},{2,130},{1... | collective-permute-start | bytes 786440 | tf_op jit(solution)/shard_map/while/body/eval_jaxpr/ppermute | solution.py:16
  265.8 163.3 %all-gather.8.cloned.1.call-start = ((), (), s32[]{:S(2)}) async-start(), calls=%async_computation.3 | async-start | bytes 6144000 | tf_op jit(solution)/shard_map/all_gather | solution.py:153
  266.1 6.0 %copy-start.4 = (bf16[196,256]{1,0:T(8,128)(2,1)S(1)}, bf16[196,256]{1,0:T(8,128)(2,1)}, u32[]{:S(2)}) copy-start(bf16[196,256]{1,0:T(8,128)(2,1)} %param.28) | copy-start | bytes 301060
  328.2 12.1 %copy-start.9 = (bf16[512,256]{1,0:T(8,128)(2,1)S(1)}, bf16[512,256]{1,0:T(8,128)(2,1)}, u32[]{:S(2)}) copy-start(bf16[512,256]{1,0:T(8,128)(2,1)} %param.27) | copy-start | bytes 786436
  362.8 3.1 copy-start.2
  443.3 1.0 copy-start.3
  443.3 28.0 %copy-start.8 = (s32[1,4]{1,0:T(1,128)S(1)}, s32[1,4]{1,0:T(1,128)}, u32[]{:S(2)}) copy-start(s32[1,4]{1,0:T(1,128)} %param.33) | copy-start | bytes 52
  462.3 10.8 %collective-permute-start.1 = (f32[1,1024]{1,0:T(1,128)S(1)}, f32[1,1024]{1,0:T(1,128)S(1)}, u32[]{:S(2)}, u32[]{:S(2)}) collective-permute-start(f32[1,1024]{1,0:T(1,128)S(1)} %get-tuple-element.418), channel_id=1, source_target_pairs={{0,1},{1,2},{2,3},{3,4},{4,5},{5,6},{6,7},{7,8},{8,9},{9,10},{10,1... | collective-permute-start | bytes 12296 | tf_op jit(solution)/shard_map/ppermute | solution.py:29
  464.3 8.9 %collective-permute-start.2 = (f32[1,1024]{1,0:T(1,128)S(1)}, f32[1,1024]{1,0:T(1,128)S(1)}, u32[]{:S(2)}, u32[]{:S(2)}) collective-permute-start(f32[1,1024]{1,0:T(1,128)S(1)} %get-tuple-element.417), channel_id=1, source_target_pairs={{1,0},{2,1},{3,2},{4,3},{5,4},{6,5},{7,6},{8,7},{9,8},{10,9},{11,1... | collective-permute-start | bytes 12296 | tf_op jit(solution)/shard_map/ppermute | solution.py:32
Sparse Core Ops, SparseCore 0:
  10.5 86.1 all-gather.3
  99.8 79.7 all-gather.5
  265.9 62.2 all-reduce.4
  366.0 63.1 all-gather.7
where the time goes:
time: 482 us; the launch traced here: 481 us
  waiting for transfers between devices  255 us (53%)
  local copies, waits for them, and re-layouts  85.6 us (18%)
  starting transfers between devices  45.1 us (9%)
  blocking collectives  32.7 us (7%)
  matrix products  25.5 us (5%)
  other arithmetic  22.2 us (5%)
  between operations  14.8 us (3%)
    all_gather x1, waiting for transfers between devices, per_device(): lax.all_gather(det_out, 'rep', axis=1, tiled=True)  79 us
    all_gather x1, waiting for transfers between devices, per_device(): attn_in = lax.all_gather(attn_part, 'section', axis=2, tiled=True)  61.6 us
    psum x1, waiting for transfers between devices, spread(): return lax.psum(kept, axis)  52.9 us
    gather x36, local copies, waits for them, and re-layouts  52 us
    ppermute x5, starting transfers between devices, passed_along(): return lax.ppermute(block, axis, route)  35.9 us
    all_gather x1, waiting for transfers between devices, per_device(): lax.all_gather(det_in, 'rep', axis=2, tiled=True)  34.7 us
    ppermute x5, waiting for transfers between devices, passed_along(): return lax.ppermute(block, axis, route)  25.1 us
    unnamed x1, blocking collectives  16.7 us
  transfers between devices with their start and end apart: 11, of which 9 were waited for; matrix products, arithmetic and copies ran while one was open for 15% of the time, Pallas kernels for 0%

commit v1 on v0

--- a/solution.py
+++ b/solution.py
@@ -150,7 +150,14 @@
     attn_part = (
         (widened - row_mean[..., None]) * lax.rsqrt(row_var[..., None] + epsilon) * gain_first
     ).astype(jnp.bfloat16)
-    attn_in = lax.all_gather(attn_part, "section", axis=2, tiled=True)
+    n_dev = lax.axis_size("section")
+    route_2 = [(i_2, (i_2 + 1) % n_dev) for i_2 in range(n_dev)]
+    parts = [attn_part]
+    for far in range(1, n_dev):
+        parts = [lax.ppermute(parts[0], "section", route_2), *parts]
+    out = jnp.concatenate(parts, axis=2)
+    shift = (lax.axis_index("section") + 1) * parts[-1].shape[2]
+    attn_in = jnp.roll(out, shift, axis=2)
     qkv = jnp.einsum("crd,de->cre", attn_in, qkv_flat, preferred_element_type=jnp.float32).astype(
         jnp.bfloat16
     )

time: 482 us -> 501 us (1.039)
  local copies, waits for them, and re-layouts: 85.6 us -> 94.3 us
  waiting for transfers between devices: 255 us -> 262 us
  starting transfers between devices: 45.1 us -> 50.6 us
    ppermute x0 -> x3, waiting for transfers between devices: none -> 70.2 us  [per_device(): parts = [lax.ppermute(parts[0], 'section', route_2), *parts]]
    all_gather x1 -> x0, waiting for transfers between devices: 61.6 us -> none  [per_device(): attn_in = lax.all_gather(attn_part, 'section', axis=2, tiled=True)]
    unnamed x25 -> x35, local copies, waits for them, and re-layouts: 4.14 us -> 13.6 us
    ppermute x0 -> x3, starting transfers between devices: none -> 5.74 us  [per_device(): parts = [lax.ppermute(parts[0], 'section', route_2), *parts]]
  transfers between devices with their start and end apart: 11 -> 13, of which waited for: 9 -> 11; matrix products, arithmetic and copies ran while one was open for 15% -> 15% of each run, Pallas kernels for 0% -> 0%
where the time goes in v1:
time: 501 us; the launch traced here: 499 us
  waiting for transfers between devices  262 us (52%)
  local copies, waits for them, and re-layouts  94.3 us (19%)
  starting transfers between devices  50.6 us (10%)
  blocking collectives  30.7 us (6%)
  matrix products  23.8 us (5%)
  other arithmetic  22.1 us (4%)
  between operations  14.8 us (3%)
    all_gather x1, waiting for transfers between devices, per_device(): lax.all_gather(det_out, 'rep', axis=1, tiled=True)  78.9 us
    ppermute x3, waiting for transfers between devices, per_device(): parts = [lax.ppermute(parts[0], 'section', route_2), *parts]  70.2 us
    psum x1, waiting for transfers between devices, spread(): return lax.psum(kept, axis)  51.7 us
    gather x36, local copies, waits for them, and re-layouts  51.6 us
    ppermute x5, starting transfers between devices, passed_along(): return lax.ppermute(block, axis, route)  35.9 us
    all_gather x1, waiting for transfers between devices, per_device(): lax.all_gather(det_in, 'rep', axis=2, tiled=True)  35.1 us
    ppermute x5, waiting for transfers between devices, passed_along(): return lax.ppermute(block, axis, route)  25.1 us
    psum x1, blocking collectives, per_device(): lax.psum((jnp.sum(widened, axis=-1), jnp.sum(widened * widened, axis=-1))...  16.1 us
  transfers between devices with their start and end apart: 13, of which 11 were waited for; matrix products, arithmetic and copies ran while one was open for 15% of the time, Pallas kernels for 0%

profile of v1, /device:TPU:32, one launch (start us, length us, event | category | flops | bytes accessed | tf_op | source)
XLA Modules:
  0.0 499.2 jit_solution(12372232525587960163)
XLA Ops:
  9.9 51.6 %while.18 = (s32[]{:T(128)}, bf16[2,16,16,768]{3,2,1,0:T(8,128)(2,1)}, s32[12,4]{0,1:T(4,128)S(1)}, bf16[12,1,14,14,768]{4,3,2,1,0:T(8,128)(2,1)}, s32[]{:T(128)}) while((s32[]{:T(128)}, bf16[2,16,16,768]{3,2,1,0:T(8,128)(2,1)}, s32[12,4]{0,1:T(4,128)S(1)}, bf16[12,1,14,14,768]{4,3,2,1,0:T(8,128)(2,1)}, s32[]{:T(128)}) %tuple.126), condition=%wide.while_cond, body=%wide.while_body.sunk | while | flops 2 | bytes 690297 | solution.py:130
  61.6 35.1 %all-gather.3.cloned.1.call-done = bf16[1,512,2048]{1,2,0:T(8,128)(2,1)} async-done(((bf16[1,512,16]{1,2,0:T(8,128)(2,1)}), bf16[1,512,2048]{1,2,0:T(8,128)(2,1)}) %all-gather.3.cloned.1.call-update) | async-done | bytes 2097168 | tf_op jit(solution)/shard_map/all_gather | solution.py:84
  100.7 78.9 %all-gather.5.cloned.1.call-done = bf16[1,2048,512]{2,1,0:T(8,128)(2,1)} async-done(((bf16[1,16,512]{2,1,0:T(8,128)(2,1)}), bf16[1,2048,512]{2,1,0:T(8,128)(2,1)}) %all-gather.5.cloned.1.call-update) | async-done | bytes 2097168 | tf_op jit(solution)/shard_map/all_gather | solution.py:85
  179.7 84.6 %while.17 = (s32[]{:T(128)}, bf16[16,16,512]{2,1,0:T(8,128)(2,1)S(1)}, bf16[2,16,16,512]{3,2,1,0:T(8,128)(2,1)S(1)}, s32[]{:T(128)}, pred[]{:T(512)}, /*index=5*...) while((s32[]{:T(128)}, ...), condition=%wide.region_5.6_spmd, body=%wide.region_0.5_spmd.sunk | while | flops 1093009664 | bytes 12373336 | solution.py:116
  179.7 10.4 %conditional.2 = (bf16[16,16,512]{2,1,0:T(8,128)(2,1)}, bf16[1,16,16,512]{3,2,1,0:T(8,128)(2,1)S(1)}) conditional(s32[]{:T(128)} %convert_element_type.78, () %tuple.120, (pred[]{:T(512)}, bf16[2,16,16,512]{3,2,1,0:T(8,128)(2,1)S(1)}, s32[]{:T(128)}, bf16[16,16,512]{2,1,0:T(8,128)(2,1)S(1)}, f32[1,512]{1,0:T(1,128)S(1)}, ...), branch_computations={%region_1.1_spmd, %region_2.4_spmd} | conditional | flops 1092878592 | bytes 10538005 | solution.py:106
  191.5 6.5 %collective-permute-done = bf16[16,16,512]{2,1,0:T(8,128)(2,1)S(1)} collective-permute-done((bf16[16,16,512]{2,1,0:T(8,128)(2,1)}, bf16[16,16,512]{2,1,0:T(8,128)(2,1)S(1)}, u32[]{:S(2)}, u32[]{:S(2)}) %collective-permute-start) | collective-permute-done | bytes 262176 | tf_op jit(solution)/shard_map/while/body/eval_jaxpr/ppermute | solution.py:16
  198.0 10.3 %conditional.2 = (bf16[16,16,512]{2,1,0:T(8,128)(2,1)}, bf16[1,16,16,512]{3,2,1,0:T(8,128)(2,1)S(1)}) conditional(s32[]{:T(128)} %convert_element_type.78, () %tuple.120, (pred[]{:T(512)}, bf16[2,16,16,512]{3,2,1,0:T(8,128)(2,1)S(1)}, s32[]{:T(128)}, bf16[16,16,512]{2,1,0:T(8,128)(2,1)S(1)}, f32[1,512]{1,0:T(1,128)S(1)}, ...), branch_computations={%region_1.1_spmd, %region_2.4_spmd} | conditional | flops 1092878592 | bytes 10538005 | solution.py:106
  208.3 4.3 collective-permute-start
  212.7 5.7 %collective-permute-done = bf16[16,16,512]{2,1,0:T(8,128)(2,1)S(1)} collective-permute-done((bf16[16,16,512]{2,1,0:T(8,128)(2,1)}, bf16[16,16,512]{2,1,0:T(8,128)(2,1)S(1)}, u32[]{:S(2)}, u32[]{:S(2)}) %collective-permute-start) | collective-permute-done | bytes 262176 | tf_op jit(solution)/shard_map/while/body/eval_jaxpr/ppermute | solution.py:16
  219.2 13.8 %collective-permute-start = (bf16[16,16,512]{2,1,0:T(8,128)(2,1)}, bf16[16,16,512]{2,1,0:T(8,128)(2,1)S(1)}, u32[]{:S(2)}, u32[]{:S(2)}) collective-permute-start(bf16[16,16,512]{2,1,0:T(8,128)(2,1)} %get-tuple-element.531), channel_id=1, source_target_pairs={{0,128},{128,256},{256,384},{1,129},{129,257},{257,385},{2,130},{1... | collective-permute-start | bytes 786440 | tf_op jit(solution)/shard_map/while/body/eval_jaxpr/ppermute | solution.py:16
  233.1 4.8 collective-permute-done
  238.7 4.3 collective-permute-start
  248.0 12.2 %collective-permute-start = (bf16[16,16,512]{2,1,0:T(8,128)(2,1)}, bf16[16,16,512]{2,1,0:T(8,128)(2,1)S(1)}, u32[]{:S(2)}, u32[]{:S(2)}) collective-permute-start(bf16[16,16,512]{2,1,0:T(8,128)(2,1)} %get-tuple-element.531), channel_id=1, source_target_pairs={{0,128},{128,256},{256,384},{1,129},{129,257},{257,385},{2,130},{1... | collective-permute-start | bytes 786440 | tf_op jit(solution)/shard_map/while/body/eval_jaxpr/ppermute | solution.py:16
  265.8 6.1 %reshape.115 = bf16[12,196,768]{2,1,0:T(8,128)(2,1)} reshape(bf16[12,1,14,14,768]{4,3,2,1,0:T(8,128)(2,1)} %get-tuple-element.289) | data formatting | bytes 7225344 | tf_op jit(solution)/shard_map/vmap()/reshape | solution.py:132
  272.0 4.6 fusion.128
  276.6 51.7 %all-reduce.5.cloned.1.call-done = bf16[2,16,16,512]{3,0,2,1:T(2,128)(2,1)} async-done(((bf16[2,16,16,512]{3,0,2,1:T(2,128)(2,1)}), bf16[2,16,16,512]{3,0,2,1:T(2,128)(2,1)}) %all-reduce.5.cloned.1.call-update) | async-done | bytes 524304 | tf_op jit(solution)/shard_map/psum | solution.py:21
  328.3 11.7 %gather_fusion = bf16[12,14,14,512]{3,0,2,1:T(8,128)(2,1)} fusion(bf16[2,16,16,512]{3,0,2,1:T(2,128)(2,1)} %all-reduce.5.cloned.1.call-done, s32[12]{0:T(128)S(1)} %get-tuple-element.423), kind=kCustom, calls=%fused_computation | custom fusion | bytes 4817088 | tf_op jit(solution)/shard_map/vmap()/gather | solution.py:133
  340.0 5.8 %fusion.134 = (f32[12,256]{1,0:T(8,128)S(1)}, f32[12,196]{1,0:T(8,128)S(1)}, f32[12,196]{1,0:T(8,128)S(1)}, f32[12,196,256]{2,1,0:T(8,128)S(1)}) fusion(f32[196,256]{1,0:T(8,128)S(1)} %convert_element_type.50, f32[12,196,256]{2,1,0:T(8,128)} %fusion.128, bf16[512,256]{1,0:T(8,128)(2,1)S(1)} %copy-done.11, bf16[12,196,512]{2,0,1:T(8,128)(2,1)} %bitcast.130), kind=kOutput, calls=%fused_computation.225 | convolution fusion | flops 620167552 | bytes 7719296 | tf_op jit(solution)/shard_map/crp,pd->crd/dot_general | solution.py:142
  345.8 16.1 %all-reduce.2 = (f32[12,196]{1,0:T(8,128)S(1)}, f32[12,196]{1,0:T(8,128)S(1)}) all-reduce(f32[12,196]{1,0:T(8,128)S(1)} %get-tuple-element.327, f32[12,196]{1,0:T(8,128)S(1)} %get-tuple-element.328), channel_id=1, replica_groups=mesh['section'=4,'rep'=128] {'section'}, use_global_device_ids=true, to_apply=%region_10.11 | all-reduce | flops 4704 | bytes 37632 | tf_op jit(solution)/shard_map/psum | solution.py:145
  364.7 25.1 %collective-permute-done.1 = bf16[12,196,256]{2,1,0:T(8,128)(2,1)S(1)} collective-permute-done((bf16[12,196,256]{2,1,0:T(8,128)(2,1)S(1)}, bf16[12,196,256]{2,1,0:T(8,128)(2,1)S(1)}, u32[]{:S(2)}, u32[]{:S(2)}) %collective-permute-start.1) | collective-permute-done | bytes 1204256 | tf_op jit(solution)/shard_map/ppermute | solution.py:157
  392.8 25.1 %collective-permute-done.2 = bf16[12,196,256]{2,1,0:T(8,128)(2,1)} collective-permute-done((bf16[12,196,256]{2,1,0:T(8,128)(2,1)S(1)}, bf16[12,196,256]{2,1,0:T(8,128)(2,1)}, u32[]{:S(2)}, u32[]{:S(2)}) %collective-permute-start.2) | collective-permute-done | bytes 1204256 | tf_op jit(solution)/shard_map/ppermute | solution.py:157
  423.4 20.0 %collective-permute-done.3 = bf16[12,196,256]{2,1,0:T(8,128)(2,1)} collective-permute-done((bf16[12,196,256]{2,1,0:T(8,128)(2,1)}, bf16[12,196,256]{2,1,0:T(8,128)(2,1)}, u32[]{:S(2)}, u32[]{:S(2)}) %collective-permute-start.3) | collective-permute-done | bytes 1204256 | tf_op jit(solution)/shard_map/ppermute | solution.py:157
  464.7 14.7 %all-reduce.1 = f32[4,3072]{1,0:T(4,128)S(1)} all-reduce(f32[4,3072]{1,0:T(4,128)S(1)} %reshape.119), channel_id=2, replica_groups=mesh['section'=4,'rep'=128] {'section'}, use_global_device_ids=true, to_apply=%region_15.16.clone | all-reduce | flops 12288 | bytes 98304
  482.4 7.0 %collective-permute-start.5 = (f32[1,1024]{1,0:T(1,128)S(1)}, f32[1,1024]{1,0:T(1,128)S(1)}, u32[]{:S(2)}, u32[]{:S(2)}) collective-permute-start(f32[1,1024]{1,0:T(1,128)S(1)} %get-tuple-element.417), channel_id=1, source_target_pairs={{1,0},{2,1},{3,2},{4,3},{5,4},{6,5},{7,6},{8,7},{9,8},{10,9},{11,1... | collective-permute-start | bytes 12296 | tf_op jit(solution)/shard_map/ppermute | solution.py:32
  (159 shorter events, 132.9 us)
Async XLA Ops:
  6.5 265.4 %copy-start = (bf16[768,256]{1,0:T(8,128)(2,1)S(1)}, bf16[768,256]{1,0:T(8,128)(2,1)}, u32[]{:S(2)}) copy-start(bf16[768,256]{1,0:T(8,128)(2,1)} %param.26) | copy-start | bytes 1179652
  6.5 90.1 %all-gather.3.cloned.1.call-start = ((), (), s32[]{:S(2)}) async-start(), calls=%async_computation | async-start | bytes 2113536 | tf_op jit(solution)/shard_map/all_gather | solution.py:84
  7.3 172.3 %all-gather.5.cloned.1.call-start = ((), (), s32[]{:S(2)}) async-start(), calls=%async_computation.1 | async-start | bytes 2113536 | tf_op jit(solution)/shard_map/all_gather | solution.py:85
  8.0 320.3 %all-reduce.5.cloned.1.call-start = ((), (), s32[]{:S(2)}) async-start(), calls=%async_computation.2 | async-start | bytes 1048576 | tf_op jit(solution)/shard_map/psum | solution.py:21
  96.6 83.1 %copy-start.3 = (bf16[2,16,16,512]{3,2,1,0:T(8,128)(2,1)S(1)}, bf16[2,16,16,512]{3,2,1,0:T(8,128)(2,1)}, u32[]{:S(2)}) copy-start(bf16[2,16,16,512]{3,2,1,0:T(8,128)(2,1)} %param.19) | copy-start | bytes 1572868
  96.6 83.1 %copy-start.7 = (f32[1,512]{1,0:T(1,128)S(1)}, f32[1,512]{1,0:T(1,128)}, u32[]{:S(2)}) copy-start(f32[1,512]{1,0:T(1,128)} %param.25) | copy-start | bytes 6148
  96.6 83.1 %copy-start.8 = (f32[1,512]{1,0:T(1,128)S(1)}, f32[1,512]{1,0:T(1,128)}, u32[]{:S(2)}) copy-start(f32[1,512]{1,0:T(1,128)} %param.22) | copy-start | bytes 6148
  179.7 86.1 %copy-start.9 = (f32[2,1024]{1,0:T(2,128)S(1)}, f32[2,1024]{1,0:T(2,128)}, u32[]{:S(2)}) copy-start(f32[2,1024]{1,0:T(2,128)} %param.31) | copy-start | bytes 24580
  190.1 7.9 %collective-permute-start = (bf16[16,16,512]{2,1,0:T(8,128)(2,1)}, bf16[16,16,512]{2,1,0:T(8,128)(2,1)S(1)}, u32[]{:S(2)}, u32[]{:S(2)}) collective-permute-start(bf16[16,16,512]{2,1,0:T(8,128)(2,1)} %get-tuple-element.531), channel_id=1, source_target_pairs={{0,128},{128,256},{256,384},{1,129},{129,257},{257,385},{2,130},{1... | collective-permute-start | bytes 786440 | tf_op jit(solution)/shard_map/while/body/eval_jaxpr/ppermute | solution.py:16
  208.3 10.1 %collective-permute-start = (bf16[16,16,512]{2,1,0:T(8,128)(2,1)}, bf16[16,16,512]{2,1,0:T(8,128)(2,1)S(1)}, u32[]{:S(2)}, u32[]{:S(2)}) collective-permute-start(bf16[16,16,512]{2,1,0:T(8,128)(2,1)} %get-tuple-element.531), channel_id=1, source_target_pairs={{0,128},{128,256},{256,384},{1,129},{129,257},{257,385},{2,130},{1... | collective-permute-start | bytes 786440 | tf_op jit(solution)/shard_map/while/body/eval_jaxpr/ppermute | solution.py:16
  219.2 18.7 %collective-permute-start = (bf16[16,16,512]{2,1,0:T(8,128)(2,1)}, bf16[16,16,512]{2,1,0:T(8,128)(2,1)S(1)}, u32[]{:S(2)}, u32[]{:S(2)}) collective-permute-start(bf16[16,16,512]{2,1,0:T(8,128)(2,1)} %get-tuple-element.531), channel_id=1, source_target_pairs={{0,128},{128,256},{256,384},{1,129},{129,257},{257,385},{2,130},{1... | collective-permute-start | bytes 786440 | tf_op jit(solution)/shard_map/while/body/eval_jaxpr/ppermute | solution.py:16
  238.7 8.5 %collective-permute-start = (bf16[16,16,512]{2,1,0:T(8,128)(2,1)}, bf16[16,16,512]{2,1,0:T(8,128)(2,1)S(1)}, u32[]{:S(2)}, u32[]{:S(2)}) collective-permute-start(bf16[16,16,512]{2,1,0:T(8,128)(2,1)} %get-tuple-element.531), channel_id=1, source_target_pairs={{0,128},{128,256},{256,384},{1,129},{129,257},{257,385},{2,130},{1... | collective-permute-start | bytes 786440 | tf_op jit(solution)/shard_map/while/body/eval_jaxpr/ppermute | solution.py:16
  248.0 16.4 %collective-permute-start = (bf16[16,16,512]{2,1,0:T(8,128)(2,1)}, bf16[16,16,512]{2,1,0:T(8,128)(2,1)S(1)}, u32[]{:S(2)}, u32[]{:S(2)}) collective-permute-start(bf16[16,16,512]{2,1,0:T(8,128)(2,1)} %get-tuple-element.531), channel_id=1, source_target_pairs={{0,128},{128,256},{256,384},{1,129},{129,257},{257,385},{2,130},{1... | collective-permute-start | bytes 786440 | tf_op jit(solution)/shard_map/while/body/eval_jaxpr/ppermute | solution.py:16
  265.8 6.1 %copy-start.6 = (bf16[196,256]{1,0:T(8,128)(2,1)S(1)}, bf16[196,256]{1,0:T(8,128)(2,1)}, u32[]{:S(2)}) copy-start(bf16[196,256]{1,0:T(8,128)(2,1)} %param.28) | copy-start | bytes 301060
  328.3 11.7 %copy-start.11 = (bf16[512,256]{1,0:T(8,128)(2,1)S(1)}, bf16[512,256]{1,0:T(8,128)(2,1)}, u32[]{:S(2)}) copy-start(bf16[512,256]{1,0:T(8,128)(2,1)} %param.27) | copy-start | bytes 786436
  362.8 27.1 %collective-permute-start.1 = (bf16[12,196,256]{2,1,0:T(8,128)(2,1)S(1)}, bf16[12,196,256]{2,1,0:T(8,128)(2,1)S(1)}, u32[]{:S(2)}, u32[]{:S(2)}) collective-permute-start(bf16[12,196,256]{2,1,0:T(8,128)(2,1)S(1)} %multiply_convert_fusion.1), channel_id=1, source_target_pairs={{0,128},{128,256},{256,384},{384,0},{1,129},{129,257},{257,385},{3... | collective-permute-start | bytes 3612680 | tf_op jit(solution)/shard_map/ppermute | solution.py:157
  389.8 1.1 copy-start.1
  390.9 27.0 %collective-permute-start.2 = (bf16[12,196,256]{2,1,0:T(8,128)(2,1)S(1)}, bf16[12,196,256]{2,1,0:T(8,128)(2,1)}, u32[]{:S(2)}, u32[]{:S(2)}) collective-permute-start(bf16[12,196,256]{2,1,0:T(8,128)(2,1)S(1)} %collective-permute-done.1), channel_id=1, source_target_pairs={{0,128},{128,256},{256,384},{384,0},{1,129},{129,257},{257,385},{3... | collective-permute-start | bytes 3612680 | tf_op jit(solution)/shard_map/ppermute | solution.py:157
  417.9 25.6 %collective-permute-start.3 = (bf16[12,196,256]{2,1,0:T(8,128)(2,1)}, bf16[12,196,256]{2,1,0:T(8,128)(2,1)}, u32[]{:S(2)}, u32[]{:S(2)}) collective-permute-start(bf16[12,196,256]{2,1,0:T(8,128)(2,1)} %collective-permute-done.2), channel_id=1, source_target_pairs={{0,128},{128,256},{256,384},{384,0},{1,129},{129,257},{257,385},{3... | collective-permute-start | bytes 3612680 | tf_op jit(solution)/shard_map/ppermute | solution.py:157
  423.4 22.9 %copy-start.2 = (bf16[12,196,256]{2,1,0:T(8,128)(2,1)S(1)}, bf16[12,196,256]{2,1,0:T(8,128)(2,1)}, u32[]{:S(2)}) copy-start(bf16[12,196,256]{2,1,0:T(8,128)(2,1)} %copy-done.1) | copy-start | bytes 3612676
  450.7 1.1 copy-start.4
  463.5 25.9 %copy-start.10 = (s32[1,4]{1,0:T(1,128)S(1)}, s32[1,4]{1,0:T(1,128)}, u32[]{:S(2)}) copy-start(s32[1,4]{1,0:T(1,128)} %param.33) | copy-start | bytes 52
  480.5 10.9 %collective-permute-start.4 = (f32[1,1024]{1,0:T(1,128)S(1)}, f32[1,1024]{1,0:T(1,128)S(1)}, u32[]{:S(2)}, u32[]{:S(2)}) collective-permute-start(f32[1,1024]{1,0:T(1,128)S(1)} %get-tuple-element.418), channel_id=1, source_target_pairs={{0,1},{1,2},{2,3},{3,4},{4,5},{5,6},{6,7},{7,8},{8,9},{9,10},{10,1... | collective-permute-start | bytes 12296 | tf_op jit(solution)/shard_map/ppermute | solution.py:29
  482.4 8.9 %collective-permute-start.5 = (f32[1,1024]{1,0:T(1,128)S(1)}, f32[1,1024]{1,0:T(1,128)S(1)}, u32[]{:S(2)}, u32[]{:S(2)}) collective-permute-start(f32[1,1024]{1,0:T(1,128)S(1)} %get-tuple-element.417), channel_id=1, source_target_pairs={{1,0},{2,1},{3,2},{4,3},{5,4},{6,5},{7,6},{8,7},{9,8},{10,9},{11,1... | collective-permute-start | bytes 12296 | tf_op jit(solution)/shard_map/ppermute | solution.py:32
  (1 other events, 1.0 us)
Sparse Core Ops, SparseCore 0:
  10.5 86.0 all-gather.2
  99.7 79.7 all-gather.4
  265.9 62.3 all-reduce.4
